TPU v7x, 32 devices: a whole 2x2x4 slice. The times are simulated.
32 devices in a mesh: section: 2 (over core), expert: 4 (over y, x), tensor: 4 (over z).
Axes of the slice: x: 2, y: 2, z: 4, core: 2. Of those that a mesh axis runs over, the one named last changes fastest.
Arguments:
- inputs: float32 [1, 788, 768], P(None, 'expert'), may hold values from -6 to 6
- cotangent: float32 [1, 788, 768], P(None, 'expert'), may hold values from -6 to 6
- norm_scale: float32 [2, 2, 768], P('section'), may hold values from 0.5 to 1.5
- norm_shift: float32 [2, 2, 768], P('section'), may hold values from -3 to 3
- proj_weight: bfloat16 [2, 768, 3, 768], P('section', None, None, 'tensor'), may hold values from -0.21875 to 0.21875
- proj_bias: float32 [2, 2, 768], P('section', None, 'tensor'), may hold values from -3 to 3
- attn_weight: bfloat16 [2, 768, 768], P('section', 'tensor'), may hold values from -0.75 to 0.75
- attn_bias: float32 [2, 768], P('section'), may hold values from -3 to 3
- expert_in: bfloat16 [2, 4, 768, 3072], P('section', 'expert', None, 'tensor'), may hold values from -0.21875 to 0.21875
- expert_in_bias: float32 [2, 4, 3072], P('section', 'expert', 'tensor'), may hold values from -3 to 3
- expert_out: bfloat16 [2, 4, 3072, 768], P('section', 'expert', 'tensor'), may hold values from -0.109375 to 0.109375
- expert_out_bias: float32 [2, 4, 768], P('section', 'expert'), may hold values from -3 to 3
- routes: int32 [2, 1, 788, 2], P('section', None, 'expert'), may hold values from 0 to 3, all different within a row; in each aligned block of 197 rows (0 to 196, 197 to 393, ..., all dimensions but the last counted through in order) at most 148 rows name the same one
- gate_weights: float32 [2, 1, 788, 2], P('section', None, 'expert'), may hold values from 0.1 to 1
Outputs:
- section_out: float32 [2, 1, 788, 768], P('section', None, 'expert')
- section_in_grad: float32 [2, 1, 788, 768], P('section', None, 'expert')
- grad_norm_scale: float32 [2, 2, 768], P('section')
- grad_norm_shift: float32 [2, 2, 768], P('section')
- grad_proj_weight: float32 [2, 768, 3, 768], P('section', None, None, 'tensor')
- grad_proj_bias: float32 [2, 2, 768], P('section', None, 'tensor')
- grad_attn_weight: float32 [2, 768, 768], P('section', 'tensor')
- grad_attn_bias: float32 [2, 768], P('section')
- grad_expert_in: float32 [2, 4, 768, 3072], P('section', 'expert', None, 'tensor')
- grad_expert_in_bias: float32 [2, 4, 3072], P('section', 'expert', 'tensor')
- grad_expert_out: float32 [2, 4, 3072, 768], P('section', 'expert', 'tensor')
- grad_expert_out_bias: float32 [2, 4, 768], P('section', 'expert')
Inputs may be any that keep to these rules, and one draw needn't show every extreme that they name: `routes`: each row names 2 different experts. In the rows of one index of the expert axis for one section and micro-batch, no expert is named more than 148 times, and in every draw some expert is named exactly 148 times there.
All inputs are finite; a program needn't handle non-finite values.
Results may differ from a plain program's by a relative error of at most 0.015.
Values may be sent and summed in bfloat16 or wider, within the bound.
A program may use at most 128 MiB of HBM per device.

v0:
```python
import jax
import jax.numpy as jnp
from jax import lax
from jax.sharding import PartitionSpec as P

HEAD_DIM = 64
SEQ = 197
TOPK = 2
NORM_EPSILON = 1e-06
GELU_FACTOR = 0.7978845608028654
CUBIC_TERM = 0.044715


def from_behind(block, axis, distance):
    devices = range(lax.axis_size(axis))
    route = [(i - distance, i) for i in devices if i - distance in devices]
    return lax.ppermute(block, axis, route)


def gelu_value(pre_act):
    inner_arg = GELU_FACTOR * (pre_act + CUBIC_TERM * pre_act * pre_act * pre_act)
    return 0.5 * pre_act * (1.0 + jnp.tanh(inner_arg))


def gelu_slope(pre_act):
    tangent = jnp.tanh(GELU_FACTOR * (pre_act + CUBIC_TERM * pre_act * pre_act * pre_act))
    return 0.5 * (1.0 + tangent) + 0.5 * pre_act * (1.0 - tangent * tangent) * GELU_FACTOR * (
        1.0 + 3.0 * CUBIC_TERM * pre_act * pre_act
    )


def layer_norm(values, scale_row, shift_row):
    average = jnp.mean(values, axis=-1, keepdims=True)
    centred = values - average
    variance = jnp.mean(centred * centred, axis=-1, keepdims=True)
    inv_std = lax.rsqrt(variance + NORM_EPSILON)
    normed = centred * inv_std
    return (normed * scale_row + shift_row, normed, inv_std)


def norm_back(grad_normed, normed, inv_std, scale_row):
    scaled = grad_normed * scale_row
    return (
        scaled
        - jnp.mean(scaled, axis=-1, keepdims=True)
        - normed * jnp.mean(scaled * normed, axis=-1, keepdims=True)
    ) * inv_std


def slot_table(route_rows, experts, capacity):
    flat_ids = route_rows.reshape(-1)
    onehot = (flat_ids[:, None] == jnp.arange(experts, dtype=jnp.int32)[None, :]).astype(jnp.int32)
    before = jnp.cumsum(onehot, axis=0) - onehot
    position = jnp.sum(before * onehot, axis=1)
    return flat_ids * capacity + position


def slot_count(row_count, experts):
    return max(2, (3 * TOPK * row_count + 2 * experts - 1) // (2 * experts))


def attend(query_rows, key_rows, value_rows):
    scores = jnp.einsum(
        "ishe,ithe->ihst", query_rows, key_rows, preferred_element_type=jnp.float32
    ) * HEAD_DIM ** (-0.5)
    log_total = jnp.log(jnp.sum(jnp.exp(scores), axis=-1))
    prob_rows = jnp.exp(scores - log_total[..., None]).astype(jnp.bfloat16)
    attn_mixed = jnp.einsum(
        "ihst,ithe->ishe", prob_rows, value_rows, preferred_element_type=jnp.float32
    ).astype(jnp.bfloat16)
    return (attn_mixed, log_total)


def attend_back(query_rows, key_rows, value_rows, attn_mixed, log_total, grad_mixed):
    scale_factor = HEAD_DIM ** (-0.5)
    scores = (
        jnp.einsum("ishe,ithe->ihst", query_rows, key_rows, preferred_element_type=jnp.float32)
        * scale_factor
    )
    prob_f = jnp.exp(scores - log_total[..., None])
    prob_rows = prob_f.astype(jnp.bfloat16)
    grad_values = jnp.einsum(
        "ihst,ishe->ithe", prob_rows, grad_mixed, preferred_element_type=jnp.float32
    )
    grad_probs = jnp.einsum(
        "ishe,ithe->ihst", grad_mixed, value_rows, preferred_element_type=jnp.float32
    )
    row_delta = jnp.einsum(
        "ishe,ishe->ihs", grad_mixed, attn_mixed, preferred_element_type=jnp.float32
    )
    grad_scores = (prob_f * (grad_probs - row_delta[..., None]) * scale_factor).astype(jnp.bfloat16)
    grad_query = jnp.einsum(
        "ihst,ithe->ishe", grad_scores, key_rows, preferred_element_type=jnp.float32
    )
    grad_keys = jnp.einsum(
        "ihst,ishe->ithe", grad_scores, query_rows, preferred_element_type=jnp.float32
    )
    return (grad_query, grad_keys, grad_values)


def hand_over(values, by_step):
    return from_behind(values, "section", by_step)


def forward_block(inputs, weights, route_rows, gate_rows):
    (
        norm_scale,
        norm_shift,
        proj_weight,
        proj_bias,
        attn_weight,
        attn_bias,
        expert_in,
        expert_in_bias,
        expert_out,
        expert_out_bias,
    ) = weights
    row_count, model_width = inputs.shape
    images = row_count // SEQ
    local_width = proj_weight.shape[2]
    head_shape = (images, SEQ, local_width // HEAD_DIM, HEAD_DIM)
    normed_out, normed_first, inv_first = layer_norm(inputs, norm_scale[0], norm_shift[0])
    projected = jnp.einsum(
        "rd,dkf->rkf",
        normed_out.astype(jnp.bfloat16),
        proj_weight,
        preferred_element_type=jnp.float32,
    )
    query_rows = (projected[:, 0] + proj_bias[0]).astype(jnp.bfloat16).reshape(head_shape)
    key_rows = projected[:, 1].astype(jnp.bfloat16).reshape(head_shape)
    value_rows = (projected[:, 2] + proj_bias[1]).astype(jnp.bfloat16).reshape(head_shape)
    attn_mixed, log_total = attend(query_rows, key_rows, value_rows)
    partial_value = jnp.dot(
        attn_mixed.reshape(row_count, local_width), attn_weight, preferred_element_type=jnp.float32
    )
    hidden_res = inputs + (lax.psum(partial_value, "tensor") + attn_bias)
    normed_out_b, normed_second, inv_second = layer_norm(hidden_res, norm_scale[1], norm_shift[1])
    experts = lax.axis_size("expert")
    capacity = slot_count(row_count, experts)
    slot_ids = slot_table(route_rows, experts, capacity)
    repeated = jnp.repeat(normed_out_b.astype(jnp.bfloat16), TOPK, axis=0)
    outgoing = (
        jnp.zeros((experts * capacity, model_width), jnp.bfloat16)
        .at[slot_ids]
        .set(repeated)
        .reshape(experts, capacity, model_width)
    )
    quarter = model_width // lax.axis_size("tensor")
    col_start = lax.axis_index("tensor") * quarter
    bias_part = lax.dynamic_slice_in_dim(expert_out_bias, col_start, quarter, 0)
    incoming = lax.all_to_all(outgoing, "expert", split_axis=0, concat_axis=0, tiled=True)
    pre_act = (
        jnp.einsum("snd,dh->snh", incoming, expert_in, preferred_element_type=jnp.float32)
        + expert_in_bias
    )
    activated = gelu_value(pre_act).astype(jnp.bfloat16)
    partial_out = jnp.einsum(
        "snh,hd->snd", activated, expert_out, preferred_element_type=jnp.float32
    )
    summed = lax.psum_scatter(partial_out, "tensor", scatter_dimension=2, tiled=True)
    produced, pre_act, received = ((summed + bias_part).astype(jnp.bfloat16), pre_act, incoming)
    gate_column = gate_rows.reshape(-1, 1)
    full_rows = lax.all_gather(produced, "tensor", axis=2, tiled=True)
    returned = lax.all_to_all(full_rows, "expert", split_axis=0, concat_axis=0, tiled=True)
    picked = returned.reshape(experts * capacity, model_width)[slot_ids]
    branch = jnp.sum((gate_column * picked).reshape(row_count, TOPK, model_width), axis=1)
    block_out = hidden_res + branch
    kept_state = (
        normed_first,
        inv_first,
        query_rows,
        key_rows,
        value_rows,
        attn_mixed,
        log_total,
        normed_second,
        inv_second,
        slot_ids,
        gate_rows,
        received,
        pre_act,
    )
    return (block_out, kept_state)


def backward_block(cotangent, weights, kept_state):
    (
        norm_scale,
        norm_shift,
        proj_weight,
        proj_bias,
        attn_weight,
        attn_bias,
        expert_in,
        expert_in_bias,
        expert_out,
        expert_out_bias,
    ) = weights
    (
        normed_first,
        inv_first,
        query_rows,
        key_rows,
        value_rows,
        attn_mixed,
        log_total,
        normed_second,
        inv_second,
        slot_ids,
        gate_rows,
        received,
        pre_act,
    ) = kept_state
    row_count, model_width = cotangent.shape
    experts = lax.axis_size("expert")
    capacity = pre_act.shape[1]
    local_width = proj_weight.shape[2]
    quarter = model_width // lax.axis_size("tensor")
    grad_rows = (
        (gate_rows.reshape(row_count, TOPK, 1) * cotangent[:, None, :])
        .astype(jnp.bfloat16)
        .reshape(TOPK * row_count, model_width)
    )
    outgoing = (
        jnp.zeros((experts * capacity, model_width), jnp.bfloat16)
        .at[slot_ids]
        .set(grad_rows)
        .reshape(experts, capacity, model_width)
    )
    grad_out = lax.all_to_all(outgoing, "expert", split_axis=0, concat_axis=0, tiled=True)
    activated = gelu_value(pre_act).astype(jnp.bfloat16)
    grad_expert_out = jnp.einsum(
        "snh,snd->hd", activated, grad_out, preferred_element_type=jnp.float32
    )
    grad_expert_out_bias = jnp.sum(grad_out, axis=(0, 1), dtype=jnp.float32)
    grad_pre = jnp.einsum(
        "snd,hd->snh", grad_out, expert_out, preferred_element_type=jnp.float32
    ) * gelu_slope(pre_act)
    grad_expert_in_bias = jnp.sum(grad_pre, axis=(0, 1))
    grad_pre_b = grad_pre.astype(jnp.bfloat16)
    grad_expert_in = jnp.einsum(
        "snd,snh->dh", received, grad_pre_b, preferred_element_type=jnp.float32
    )
    partial_in = jnp.einsum(
        "snh,dh->snd", grad_pre_b, expert_in, preferred_element_type=jnp.float32
    )
    grad_buffer = lax.psum_scatter(partial_in, "tensor", scatter_dimension=2, tiled=True).astype(
        jnp.bfloat16
    )
    returned = lax.all_to_all(grad_buffer, "expert", split_axis=0, concat_axis=0, tiled=True)
    picked = returned.reshape(experts * capacity, quarter)[slot_ids]
    grad_cols = jnp.sum(picked.reshape(row_count, TOPK, quarter), axis=1, dtype=jnp.float32)
    grad_normed_b = lax.all_gather(grad_cols, "tensor", axis=1, tiled=True)
    grad_hidden = cotangent + norm_back(grad_normed_b, normed_second, inv_second, norm_scale[1])
    grad_hidden_b = grad_hidden.astype(jnp.bfloat16)
    grad_attn_bias = jnp.sum(grad_hidden, axis=0)
    mixed_flat = attn_mixed.reshape(row_count, local_width)
    grad_attn_weight = jnp.einsum(
        "rf,rd->fd", mixed_flat, grad_hidden_b, preferred_element_type=jnp.float32
    )
    grad_mixed = (
        jnp.einsum("rd,fd->rf", grad_hidden_b, attn_weight, preferred_element_type=jnp.float32)
        .astype(jnp.bfloat16)
        .reshape(attn_mixed.shape)
    )
    grad_query, grad_keys, grad_values = attend_back(
        query_rows, key_rows, value_rows, attn_mixed, log_total, grad_mixed
    )
    query_flat = grad_query.reshape(row_count, local_width)
    key_flat = grad_keys.reshape(row_count, local_width)
    value_flat = grad_values.reshape(row_count, local_width)
    grad_proj_bias = jnp.stack([jnp.sum(query_flat, axis=0), jnp.sum(value_flat, axis=0)])
    grad_proj = jnp.stack([query_flat, key_flat, value_flat], axis=1).astype(jnp.bfloat16)
    normed_a = (normed_first * norm_scale[0] + norm_shift[0]).astype(jnp.bfloat16)
    grad_proj_weight = jnp.einsum(
        "rd,rkf->dkf", normed_a, grad_proj, preferred_element_type=jnp.float32
    )
    partial_norm = jnp.einsum(
        "rkf,dkf->rd", grad_proj, proj_weight, preferred_element_type=jnp.float32
    )
    grad_normed_a = lax.psum(partial_norm, "tensor")
    grad_input = grad_hidden + norm_back(grad_normed_a, normed_first, inv_first, norm_scale[0])
    grad_norm_scale = jnp.stack(
        [
            jnp.sum(grad_normed_a * normed_first, axis=0),
            jnp.sum(grad_normed_b * normed_second, axis=0),
        ]
    )
    grad_norm_shift = jnp.stack([jnp.sum(grad_normed_a, axis=0), jnp.sum(grad_normed_b, axis=0)])
    mixer_part = (
        grad_norm_scale,
        grad_norm_shift,
        grad_proj_weight,
        grad_proj_bias,
        grad_attn_weight,
        grad_attn_bias,
    )
    expert_part = (grad_expert_in, grad_expert_in_bias, grad_expert_out, grad_expert_out_bias)
    return (grad_input, mixer_part, expert_part)


def on_device(
    inputs,
    cotangent,
    norm_scale,
    norm_shift,
    proj_weight,
    proj_bias,
    attn_weight,
    attn_bias,
    expert_in,
    expert_in_bias,
    expert_out,
    expert_out_bias,
    routes,
    gate_weights,
):
    weights = (
        norm_scale[0],
        norm_shift[0],
        proj_weight[0],
        proj_bias[0],
        attn_weight[0],
        attn_bias[0],
        expert_in[0, 0],
        expert_in_bias[0, 0],
        expert_out[0, 0],
        expert_out_bias[0, 0],
    )
    section_id = lax.axis_index("section")
    is_first = section_id == 0
    micro_count = inputs.shape[0]
    received = jnp.zeros_like(inputs[0])
    saved_keeps = []
    produced = []
    for tick_index in range(micro_count + 1):
        own_micro = jnp.clip(tick_index - section_id, 0, micro_count - 1)
        block_in = jnp.where(is_first, inputs[min(tick_index, micro_count - 1)], received)
        route_rows = lax.dynamic_index_in_dim(routes[0], own_micro, 0, keepdims=False)
        gate_rows = lax.dynamic_index_in_dim(gate_weights[0], own_micro, 0, keepdims=False)
        block_out, kept_state = forward_block(block_in, weights, route_rows, gate_rows)
        saved_keeps.append(kept_state)
        produced.append(block_out)
        if tick_index < micro_count:
            received = hand_over(block_out, 1)
    sent_back = jnp.zeros_like(inputs[0])
    mixer_sums = None
    expert_sums = None
    input_grads = []
    for tick_index in range(micro_count + 1):
        last_cotangent = cotangent[min(tick_index, micro_count - 1)]
        if tick_index == micro_count:
            last_cotangent = jnp.zeros_like(last_cotangent)
        block_grad = jnp.where(is_first, sent_back, last_cotangent)
        kept_state = jax.tree.map(
            lambda later_keep, early_keep: jnp.where(is_first, early_keep, later_keep),
            saved_keeps[min(tick_index + 1, micro_count)],
            saved_keeps[max(tick_index - 1, 0)],
        )
        grad_input, mixer_part, expert_part = backward_block(block_grad, weights, kept_state)
        mixer_sums = (
            mixer_part if mixer_sums is None else jax.tree.map(jnp.add, mixer_sums, mixer_part)
        )
        expert_sums = (
            expert_part if expert_sums is None else jax.tree.map(jnp.add, expert_sums, expert_part)
        )
        input_grads.append(grad_input)
        if tick_index < micro_count:
            sent_back = hand_over(grad_input, -1)
    section_out = jnp.stack([jnp.where(is_first, produced[0], produced[1])])
    section_in_grad = jnp.stack([jnp.where(is_first, input_grads[1], input_grads[0])])
    scale_sum, shift_sum, proj_sum, proj_bias_sum, attn_sum_w, attn_bias_sum = mixer_sums
    totals = lax.psum(
        (scale_sum, shift_sum, proj_sum, proj_bias_sum, attn_sum_w, attn_bias_sum), "expert"
    )
    grad_in_w, grad_in_b, grad_out_w, grad_out_b = expert_sums
    return (
        section_out[None],
        section_in_grad[None],
        totals[0][None],
        totals[1][None],
        totals[2][None],
        totals[3][None],
        totals[4][None],
        totals[5][None],
        grad_in_w[None, None],
        grad_in_b[None, None],
        grad_out_w[None, None],
        grad_out_b[None, None],
    )


def solution(mesh):
    in_specs = (
        P(None, "expert", None),
        P(None, "expert", None),
        P("section", None, None),
        P("section", None, None),
        P("section", None, None, "tensor"),
        P("section", None, "tensor"),
        P("section", "tensor", None),
        P("section", None),
        P("section", "expert", None, "tensor"),
        P("section", "expert", "tensor"),
        P("section", "expert", "tensor", None),
        P("section", "expert", None),
        P("section", None, "expert", None),
        P("section", None, "expert", None),
    )
    out_specs = (
        P("section", None, "expert", None),
        P("section", None, "expert", None),
        P("section", None, None),
        P("section", None, None),
        P("section", None, None, "tensor"),
        P("section", None, "tensor"),
        P("section", "tensor", None),
        P("section", None),
        P("section", "expert", None, "tensor"),
        P("section", "expert", "tensor"),
        P("section", "expert", "tensor", None),
        P("section", "expert", None),
    )
    return jax.shard_map(
        on_device, mesh=mesh, in_specs=in_specs, out_specs=out_specs, check_vma=False
    )
```

profile of v0, /device:TPU:0, one launch (start us, length us, event | category | flops | bytes accessed | tf_op | source)
XLA Modules:
  0.0 782.8 jit_solution(3827961485082313167)
XLA Ops:
  18.0 40.3 %all-reduce.9.cloned.1.call-done = f32[197,768]{1,0:T(8,128)} async-done(((f32[197,768]{1,0:T(8,128)}), f32[197,768]{1,0:T(8,128)}) %all-reduce.9.cloned.1.call-update) | async-done | bytes 605200 | tf_op jit(solution)/shard_map/psum | solution.py:136
  62.0 3.0 scatter_custom_fusion
  66.1 4.2 all-to-all-start
  70.5 12.0 %all-to-all-done = bf16[4,148,768]{2,1,0:T(8,128)(2,1)} async-done(((bf16[4,148,768]{2,1,0:T(8,128)(2,1)}), bf16[4,148,768]{2,1,0:T(8,128)(2,1)}, u32[]{:S(2)}, u32[]{:S(2)}) %all-to-all-start) | async-done | bytes 909344 | tf_op jit(solution)/shard_map/all_to_all | solution.py:151
  88.5 4.3 copy.142
  92.8 4.5 reshape.717
  98.1 39.8 %reduce-scatter.13.cloned.1.call-done = f32[192,592]{1,0:T(8,128)} async-done(((f32[768,592]{1,0:T(8,128)}), f32[192,592]{1,0:T(8,128)}) %reduce-scatter.13.cloned.1.call-update) | async-done | bytes 454672
  142.2 29.4 %all_gather.12 = bf16[4,148,768]{1,0,2:T(4,128)(2,1)} all-gather(bf16[4,148,192]{1,0,2:T(4,128)(2,1)S(1)} %copy.93), channel_id=1, replica_groups=mesh['section'=2,'expert'=4,'tensor'=4] {'tensor'}, dimensions={2}, use_global_device_ids=true | all-gather | bytes 1136640 | tf_op jit(solution)/shard_map/all_gather | solution.py:163
  171.5 3.5 copy.94
  175.0 4.2 all-to-all-start.1
  180.3 9.9 %all-to-all-done.1 = bf16[4,148,768]{2,1,0:T(8,128)(2,1)} async-done(((bf16[4,148,768]{2,1,0:T(8,128)(2,1)}), bf16[4,148,768]{2,1,0:T(8,128)(2,1)}, u32[]{:S(2)}, u32[]{:S(2)}) %all-to-all-start.1) | async-done | bytes 909344 | tf_op jit(solution)/shard_map/all_to_all | solution.py:164
  207.2 40.7 %all-reduce.11.cloned.1.call-done = f32[197,768]{1,0:T(8,128)} async-done(((f32[197,768]{1,0:T(8,128)}), f32[197,768]{1,0:T(8,128)}) %all-reduce.11.cloned.1.call-update) | async-done | bytes 605200 | tf_op jit(solution)/shard_map/psum | solution.py:136
  256.4 4.8 all-to-all-start.2
  262.8 3.0 mul.457
  265.9 3.3 scatter_custom_fusion.2
  273.2 3.5 all-to-all-start.4
  276.8 4.6 multiply_convert_fusion
  281.4 7.3 all-to-all-done.4
  288.7 5.2 fusion.129
  297.0 4.3 copy.146
  301.3 4.5 reshape.721
  306.5 4.4 fusion.28
  310.9 4.3 copy.144
  315.2 4.5 reshape.719
  319.8 26.7 %reduce-scatter.17.cloned.1.call-done = f32[192,592]{1,0:T(8,128)} async-done(((f32[768,592]{1,0:T(8,128)}), f32[192,592]{1,0:T(8,128)}) %reduce-scatter.17.cloned.1.call-update) | async-done | bytes 454672
  348.8 4.1 all-to-all-start.5
  352.9 37.0 %reduce-scatter.15.cloned.1.call-done = f32[192,592]{1,0:T(8,128)} async-done(((f32[768,592]{1,0:T(8,128)}), f32[192,592]{1,0:T(8,128)}) %reduce-scatter.15.cloned.1.call-update) | async-done | bytes 454672
  394.1 29.4 %all_gather.13 = bf16[4,148,768]{1,0,2:T(4,128)(2,1)} all-gather(bf16[4,148,192]{1,0,2:T(4,128)(2,1)S(1)} %copy.96), channel_id=1, replica_groups=mesh['section'=2,'expert'=4,'tensor'=4] {'tensor'}, dimensions={2}, use_global_device_ids=true | all-gather | bytes 1136640 | tf_op jit(solution)/shard_map/all_gather | solution.py:163
  423.5 3.5 copy.97
  427.0 4.3 all-to-all-start.3
  437.4 19.4 %all_gather.14 = f32[197,768]{0,1:T(8,128)S(1)} all-gather(f32[197,192]{0,1:T(8,128)S(1)} %copy.100), channel_id=1, replica_groups=mesh['section'=2,'expert'=4,'tensor'=4] {'tensor'}, dimensions={1}, use_global_device_ids=true | all-gather | bytes 756480 | tf_op jit(solution)/shard_map/all_gather | solution.py:253
  475.6 39.6 %all-reduce.13.cloned.1.call-done = f32[197,768]{1,0:T(8,128)} async-done(((f32[197,768]{1,0:T(8,128)}), f32[197,768]{1,0:T(8,128)}) %all-reduce.13.cloned.1.call-update) | async-done | bytes 605200 | tf_op jit(solution)/shard_map/psum | solution.py:281
  524.6 3.0 mul.490
  527.6 4.0 scatter_custom_fusion.3
  533.9 17.6 %all_to_all.40 = bf16[4,148,768]{2,1,0:T(8,128)(2,1)S(1)} all-to-all(bf16[4,148,768]{2,1,0:T(8,128)(2,1)} %reshape.622), channel_id=1, replica_groups=mesh['section'=2,'expert'=4,'tensor'=4] {'expert'}, dimensions={0} | all-to-all | bytes 1818624 | tf_op jit(solution)/shard_map/all_to_all | solution.py:230
  551.5 4.9 fusion.130
  559.6 4.3 copy.148
  563.8 4.5 reshape.723
  569.8 4.2 fusion.61
  575.8 32.2 %reduce-scatter.19.cloned.1.call-done = f32[192,592]{1,0:T(8,128)} async-done(((f32[768,592]{1,0:T(8,128)}), f32[192,592]{1,0:T(8,128)}) %reduce-scatter.19.cloned.1.call-update) | async-done | bytes 454672
  610.4 3.7 all-to-all-start.7
  628.1 18.3 %all_gather.15 = f32[197,768]{0,1:T(8,128)} all-gather(f32[197,192]{0,1:T(8,128)} %copy.107), channel_id=1, replica_groups=mesh['section'=2,'expert'=4,'tensor'=4] {'tensor'}, dimensions={1}, use_global_device_ids=true | all-gather | bytes 756480 | tf_op jit(solution)/shard_map/all_gather | solution.py:253
  658.9 4.1 fusion.131
  667.4 4.4 fusion
  671.8 3.9 fusion.1
  676.0 18.1 %all-reduce.15.cloned.1.call-done = f32[197,768]{1,0:T(8,128)} async-done(((f32[197,768]{1,0:T(8,128)}), f32[197,768]{1,0:T(8,128)}) %all-reduce.15.cloned.1.call-update) | async-done | bytes 605200 | tf_op jit(solution)/shard_map/psum | solution.py:281
  698.4 17.9 %all-reduce.1 = (f32[1,2,768]{2,1,0:T(2,128)}, f32[1,2,768]{2,1,0:T(2,128)}, f32[1,2,192]{2,1,0:T(2,128)}, f32[1,768]{1,0:T(1,128)}) all-reduce(f32[1,2,768]{2,1,0:T(2,128)S(1)} %fusion.106, f32[1,2,768]{2,1,0:T(2,128)S(1)} %fusion.107, f32[1,2,192]{2,1,0:T(2,128)S(1)} %fusion.108, ...), channel_id=1, replica_groups=mesh['section'=2,'expert'=4,'tensor'=4] {'expert'}, use_global_device_ids=true, to_apply=%region_41.42 | all-reduce | flops 4224 | bytes 33792 | tf_op jit(solution)/shard_map/psum | solution.py:373
  716.3 55.8 %all-reduce.17.cloned.1.call-done = (f32[1,768,3,192]{1,3,2,0:T(8,128)}, f32[1,192,768]{2,1,0:T(8,128)}) async-done(((f32[1,768,3,192]{1,3,2,0:T(8,128)}, f32[1,192,768]{2,1,0:T(8,128)}), (f32[1,768,3,192]{1,3,2,0:T(8,128)}, f32[1,192,768]{2,1,0:T(8,128)})) %all-reduce.17.cloned.1.call-update) | async-done | bytes 2359312 | tf_op jit(solution)/shard_map/psum | solution.py:373
  (434 shorter events, 152.1 us)
Async XLA Ops:
  7.2 75.3 %copy-start = (bf16[1,1,768,768]{3,2,1,0:T(8,128)(2,1)S(1)}, bf16[1,1,768,768]{3,2,1,0:T(8,128)(2,1)}, u32[]{:S(2)}) copy-start(bf16[1,1,768,768]{3,2,1,0:T(8,128)(2,1)} %param.22) | copy-start | bytes 3538948
  7.2 51.1 %all-reduce.9.cloned.1.call-start = ((), (), s32[]{:S(2)}) async-start(), calls=%async_computation.12 | async-start | bytes 1228800 | tf_op jit(solution)/shard_map/psum | solution.py:136
  13.6 191.1 %copy-start.65 = (f32[3,64]{1,0:T(4,128)}, f32[3,64]{1,0:T(4,128)S(1)}, u32[]{:S(2)}) copy-start(f32[3,64]{1,0:T(4,128)S(1)} %add.382) | copy-start | bytes 2308
  14.0 44.3 %copy-start.2 = (f32[1,197,768]{2,0,1:T(1,128)S(1)}, f32[1,197,768]{2,0,1:T(1,128)}, u32[]{:S(2)}) copy-start(f32[1,197,768]{2,0,1:T(1,128)} %param.14) | copy-start | bytes 1815556
  14.2 45.3 %copy-start.32 = (bf16[197,3,64]{0,2,1:T(8,128)(2,1)}, bf16[197,3,64]{0,2,1:T(8,128)(2,1)S(1)}, u32[]{:S(2)}) copy-start(bf16[197,3,64]{0,2,1:T(8,128)(2,1)S(1)} %add_convert_fusion.11) | copy-start | bytes 226948
  14.4 45.1 %copy-start.54 = (bf16[3,64,197]{2,1,0:T(8,128)(2,1)}, bf16[3,64,197]{2,1,0:T(8,128)(2,1)S(1)}, u32[]{:S(2)}) copy-start(bf16[3,64,197]{2,1,0:T(8,128)(2,1)S(1)} %convolution_convert_fusion.5) | copy-start | bytes 226948
  18.0 44.1 %copy-start.95 = (s32[394,1]{0,1:T(1,128)}, s32[394,1]{0,1:T(1,128)S(1)}, u32[]{:S(2)}) copy-start(s32[394,1]{0,1:T(1,128)S(1)} %compare_select_fusion) | copy-start | bytes 4732
  66.1 16.4 %all-to-all-start = ((bf16[4,148,768]{2,1,0:T(8,128)(2,1)}), bf16[4,148,768]{2,1,0:T(8,128)(2,1)}, u32[]{:S(2)}, u32[]{:S(2)}) async-start(bf16[4,148,768]{2,1,0:T(8,128)(2,1)} %reshape.612), calls=%async_computation | async-start | bytes 1867776 | tf_op jit(solution)/shard_map/all_to_all | solution.py:151
  70.4 67.6 %reduce-scatter.13.cloned.1.call-start = ((), (), s32[]{:S(2)}) async-start(), calls=%async_computation.16 | async-start | bytes 2457600
  70.5 14.2 %copy-start.101 = (f32[768]{0:T(1024)}, f32[768]{0:T(1024)S(1)}, u32[]{:S(2)}) copy-start(f32[768]{0:T(1024)S(1)} %reduce.18) | copy-start | bytes 9220
  98.1 44.0 %copy-start.89 = (f32[1,1,192]{2,1,0:T(1,128)}, f32[1,1,192]{2,1,0:T(1,128)S(1)}, u32[]{:S(2)}) copy-start(f32[1,1,192]{2,1,0:T(1,128)S(1)} %constant_dynamic-slice_fusion) | copy-start | bytes 2308
  171.5 8.0 %copy-start.93 = (f32[1,1,197,2]{2,3,1,0:T(2,128)S(1)}, f32[1,1,197,2]{2,3,1,0:T(2,128)}, u32[]{:S(2)}) copy-start(f32[1,1,197,2]{2,3,1,0:T(2,128)} %param.27) | copy-start | bytes 4732
  171.5 8.8 %copy-start.96 = (s32[394,1]{0,1:T(1,128)S(1)}, s32[394,1]{0,1:T(1,128)}, u32[]{:S(2)}) copy-start(s32[394,1]{0,1:T(1,128)} %copy-done.95) | copy-start | bytes 4732
  175.0 15.2 %all-to-all-start.1 = ((bf16[4,148,768]{2,1,0:T(8,128)(2,1)}), bf16[4,148,768]{2,1,0:T(8,128)(2,1)}, u32[]{:S(2)}, u32[]{:S(2)}) async-start(bf16[4,148,768]{2,1,0:T(8,128)(2,1)} %copy.94), calls=%async_computation.1 | async-start | bytes 1867776 | tf_op jit(solution)/shard_map/all_to_all | solution.py:164
  179.3 68.6 %all-reduce.11.cloned.1.call-start = ((), (), s32[]{:S(2)}) async-start(), calls=%async_computation.13 | async-start | bytes 1228800 | tf_op jit(solution)/shard_map/psum | solution.py:136
  200.0 3.1 collective-permute-start
  205.8 43.3 %copy-start.34 = (bf16[197,3,64]{0,2,1:T(8,128)(2,1)}, bf16[197,3,64]{0,2,1:T(8,128)(2,1)S(1)}, u32[]{:S(2)}) copy-start(bf16[197,3,64]{0,2,1:T(8,128)(2,1)S(1)} %add_convert_fusion.9) | copy-start | bytes 226948
  206.0 43.4 %copy-start.56 = (bf16[3,64,197]{2,1,0:T(8,128)(2,1)}, bf16[3,64,197]{2,1,0:T(8,128)(2,1)S(1)}, u32[]{:S(2)}) copy-start(bf16[3,64,197]{2,1,0:T(8,128)(2,1)S(1)} %convolution_convert_fusion.4) | copy-start | bytes 226948
  206.1 43.3 %copy-start.88 = (f32[197]{0:T(256)S(1)}, f32[197]{0:T(256)}, u32[]{:S(2)}) copy-start(f32[197]{0:T(256)} %copy-done.87) | copy-start | bytes 2368
  249.2 6.1 copy-start.73
  255.2 5.9 copy-start.94
  256.4 16.9 %all-to-all-start.2 = ((bf16[4,148,768]{2,1,0:T(8,128)(2,1)}), bf16[4,148,768]{2,1,0:T(8,128)(2,1)}, u32[]{:S(2)}, u32[]{:S(2)}) async-start(bf16[4,148,768]{2,1,0:T(8,128)(2,1)} %reshape.616), calls=%async_computation.2 | async-start | bytes 1867776 | tf_op jit(solution)/shard_map/all_to_all | solution.py:151
  273.2 15.4 %all-to-all-start.4 = ((bf16[4,148,768]{2,1,0:T(8,128)(2,1)}), bf16[4,148,768]{2,1,0:T(8,128)(2,1)S(1)}, u32[]{:S(2)}, u32[]{:S(2)}) async-start(bf16[4,148,768]{2,1,0:T(8,128)(2,1)} %reshape.618), calls=%async_computation.4 | async-start | bytes 1867776 | tf_op jit(solution)/shard_map/all_to_all | solution.py:230
  276.8 69.7 %reduce-scatter.17.cloned.1.call-start = ((), (), s32[]{:S(2)}) async-start(), calls=%async_computation.18 | async-start | bytes 2457600
  305.9 84.1 %reduce-scatter.15.cloned.1.call-start = ((), (), s32[]{:S(2)}) async-start(), calls=%async_computation.17 | async-start | bytes 2457600
  347.8 44.9 %copy-start.90 = (f32[1,1,192]{2,1,0:T(1,128)S(1)}, f32[1,1,192]{2,1,0:T(1,128)}, u32[]{:S(2)}) copy-start(f32[1,1,192]{2,1,0:T(1,128)} %copy-done.89) | copy-start | bytes 2308
  348.8 78.2 %all-to-all-start.5 = ((bf16[4,148,192]{2,1,0:T(8,128)(2,1)}), bf16[4,148,192]{2,1,0:T(8,128)(2,1)}, u32[]{:S(2)}, u32[]{:S(2)}) async-start(bf16[4,148,192]{2,1,0:T(8,128)(2,1)} %copy.147), calls=%async_computation.5 | async-start | bytes 622592 | tf_op jit(solution)/shard_map/all_to_all | solution.py:250
  423.5 8.0 %copy-start.31 = (f32[197,1,192]{0,2,1:T(8,128)S(1)}, f32[197,1,192]{0,2,1:T(8,128)}, u32[]{:S(2)}) copy-start(f32[197,1,192]{0,2,1:T(8,128)} %copy-done.30) | copy-start | bytes 453892
  423.5 8.0 %copy-start.51 = (bf16[197,1,192]{0,2,1:T(8,128)(2,1)S(1)}, bf16[197,1,192]{0,2,1:T(8,128)(2,1)}, u32[]{:S(2)}) copy-start(bf16[197,1,192]{0,2,1:T(8,128)(2,1)} %copy-done.50) | copy-start | bytes 226948
  423.5 8.0 %copy-start.53 = (bf16[197,1,192]{0,2,1:T(8,128)(2,1)S(1)}, bf16[197,1,192]{0,2,1:T(8,128)(2,1)}, u32[]{:S(2)}) copy-start(bf16[197,1,192]{0,2,1:T(8,128)(2,1)} %copy-done.52) | copy-start | bytes 226948
  423.5 8.0 %copy-start.66 = (f32[3,64]{1,0:T(4,128)S(1)}, f32[3,64]{1,0:T(4,128)}, u32[]{:S(2)}) copy-start(f32[3,64]{1,0:T(4,128)} %copy-done.65) | copy-start | bytes 2308
  427.0 30.9 %all-to-all-start.3 = ((bf16[4,148,768]{2,1,0:T(8,128)(2,1)}), bf16[4,148,768]{2,1,0:T(8,128)(2,1)}, u32[]{:S(2)}, u32[]{:S(2)}) async-start(bf16[4,148,768]{2,1,0:T(8,128)(2,1)} %copy.97), calls=%async_computation.3 | async-start | bytes 1867776 | tf_op jit(solution)/shard_map/all_to_all | solution.py:164
  431.4 83.9 %all-reduce.13.cloned.1.call-start = ((), (), s32[]{:S(2)}) async-start(), calls=%async_computation.14 | async-start | bytes 1228800 | tf_op jit(solution)/shard_map/psum | solution.py:281
  461.9 5.8 copy-start.74
  461.9 5.8 copy-start.80
  462.0 5.8 copy-start.84
  472.7 42.6 %copy-start.70 = (f32[197]{0:T(256)S(1)}, f32[197]{0:T(256)}, u32[]{:S(2)}) copy-start(f32[197]{0:T(256)} %copy-done.69) | copy-start | bytes 2368
  472.7 42.6 %copy-start.77 = (f32[197]{0:T(256)S(1)}, f32[197]{0:T(256)}, u32[]{:S(2)}) copy-start(f32[197]{0:T(256)} %copy-done.76) | copy-start | bytes 2368
  475.6 132.5 %reduce-scatter.19.cloned.1.call-start = ((), (), s32[]{:S(2)}) async-start(), calls=%async_computation.19 | async-start | bytes 2457600
  518.4 9.2 %copy-start.25 = (f32[197,768]{1,0:T(8,128)}, f32[197,768]{1,0:T(8,128)S(1)}, u32[]{:S(2)}) copy-start(f32[197,768]{1,0:T(8,128)S(1)} %multiply_add_fusion.4) | copy-start | bytes 1815556
  518.4 3.9 collective-permute-start.1
  531.6 19.9 %copy-start.103 = (f32[768]{0:T(1024)S(1)}, f32[768]{0:T(1024)}, u32[]{:S(2)}) copy-start(f32[768]{0:T(1024)} %copy-done.101) | copy-start | bytes 9220
  533.9 17.7 %copy-start.108 = (bf16[1,1,768,768]{3,2,1,0:T(8,128)(2,1)S(1)}, bf16[1,1,768,768]{3,2,1,0:T(8,128)(2,1)}, u32[]{:S(2)}) copy-start(bf16[1,1,768,768]{3,2,1,0:T(8,128)(2,1)} %param.24) | copy-start | bytes 3538948
  610.4 9.2 %all-to-all-start.7 = ((bf16[4,148,192]{2,1,0:T(8,128)(2,1)}), bf16[4,148,192]{2,1,0:T(8,128)(2,1)S(1)}, u32[]{:S(2)}, u32[]{:S(2)}) async-start(bf16[4,148,192]{2,1,0:T(8,128)(2,1)} %copy.149), calls=%async_computation.7 | async-start | bytes 622592 | tf_op jit(solution)/shard_map/all_to_all | solution.py:250
  614.0 80.1 %all-reduce.15.cloned.1.call-start = ((), (), s32[]{:S(2)}) async-start(), calls=%async_computation.15 | async-start | bytes 1228800 | tf_op jit(solution)/shard_map/psum | solution.py:281
  622.2 26.4 %copy-start.8 = (f32[197,768]{1,0:T(8,128)S(1)}, f32[197,768]{1,0:T(8,128)}, u32[]{:S(2)}) copy-start(f32[197,768]{1,0:T(8,128)} %copy-done.7) | copy-start | bytes 1815556
  655.6 116.5 %all-reduce.17.cloned.1.call-start = ((), (), s32[]{:S(2)}) async-start(), calls=%async_computation.20 | async-start | bytes 4718592 | tf_op jit(solution)/shard_map/psum | solution.py:373
  675.7 19.9 %copy-start.81 = (f32[197]{0:T(256)S(1)}, f32[197]{0:T(256)}, u32[]{:S(2)}) copy-start(f32[197]{0:T(256)} %get-tuple-element.115) | copy-start | bytes 2368
  (85 other events, 243.5 us)
Sparse Core Ops, SparseCore 0:
  15.7 42.5 all-reduce.8
  97.5 40.4 reduce-scatter.12
  207.3 40.5 all-reduce.10
  306.0 40.4 reduce-scatter.16
  349.2 40.6 reduce-scatter.14
  475.7 39.5 all-reduce.12
  568.5 39.4 reduce-scatter.18
  655.7 38.4 all-reduce.14
  697.9 74.1 all-reduce.16
where the time goes:
time: 794 us; the launch traced here: 783 us
  waiting for transfers between devices  370 us (47%)
  blocking collectives  132 us (17%)
  local copies, waits for them, and re-layouts  126 us (16%)
  matrix products  63.3 us (8%)
  other arithmetic  43 us (5%)
  starting transfers between devices  32.6 us (4%)
  between operations  16.1 us (2%)
    unnamed x13, waiting for transfers between devices  136 us
    psum x2, waiting for transfers between devices, forward_block(): hidden_res = inputs + (lax.psum(partial_value, 'tensor') + attn_bias)  81 us
    unnamed x253, local copies, waits for them, and re-layouts  61.4 us
    all_gather x2, blocking collectives, forward_block(): full_rows = lax.all_gather(produced, 'tensor', axis=2, tiled=True)  58.7 us
    psum x2, waiting for transfers between devices, backward_block(): grad_normed_a = lax.psum(partial_norm, 'tensor')  57.8 us
    psum x1, waiting for transfers between devices, on_device(): lax.psum((scale_sum, shift_sum, proj_sum, proj_bias_sum, attn_sum_w, attn...  55.8 us
    all_gather x2, blocking collectives, backward_block(): grad_normed_b = lax.all_gather(grad_cols, 'tensor', axis=1, tiled=True)  37.7 us
    psum x1, blocking collectives, on_device(): lax.psum((scale_sum, shift_sum, proj_sum, proj_bias_sum, attn_sum_w, attn...  17.9 us
  transfers between devices with their start and end apart: 18, of which 16 were waited for; matrix products, arithmetic and copies ran while one was open for 10% of the time, Pallas kernels for 0%

commit v1 on v0

--- a/solution.py
+++ b/solution.py
@@ -133,7 +133,7 @@
     partial_value = jnp.dot(
         attn_mixed.reshape(row_count, local_width), attn_weight, preferred_element_type=jnp.float32
     )
-    hidden_res = inputs + (lax.psum(partial_value, "tensor") + attn_bias)
+    hidden_res = inputs + (jnp.sum(lax.all_gather(partial_value, "tensor"), axis=0) + attn_bias)
     normed_out_b, normed_second, inv_second = layer_norm(hidden_res, norm_scale[1], norm_shift[1])
     experts = lax.axis_size("expert")
     capacity = slot_count(row_count, experts)

time: 794 us -> 820 us (1.033)
  waiting for transfers between devices: 370 us -> 393 us
    all_gather x0 -> x2, waiting for transfers between devices: none -> 105 us  [forward_block(): lax.all_gather(partial_value, 'tensor')]
    psum x2 -> x0, waiting for transfers between devices: 81 us -> none  [forward_block(): hidden_res = inputs + (lax.psum(partial_value, 'tensor') + attn_bias)]
where the time goes in v1:
time: 820 us; the launch traced here: 808 us
  waiting for transfers between devices  393 us (48%)
  blocking collectives  132 us (16%)
  local copies, waits for them, and re-layouts  126 us (15%)
  matrix products  63.2 us (8%)
  other arithmetic  44.7 us (5%)
  starting transfers between devices  32.6 us (4%)
  between operations  16.1 us (2%)
    unnamed x13, waiting for transfers between devices  134 us
    all_gather x2, waiting for transfers between devices, forward_block(): lax.all_gather(partial_value, 'tensor')  105 us
    unnamed x253, local copies, waits for them, and re-layouts  61.6 us
    all_gather x2, blocking collectives, forward_block(): full_rows = lax.all_gather(produced, 'tensor', axis=2, tiled=True)  58.7 us
    psum x2, waiting for transfers between devices, backward_block(): grad_normed_a = lax.psum(partial_norm, 'tensor')  57.8 us
    psum x1, waiting for transfers between devices, on_device(): lax.psum((scale_sum, shift_sum, proj_sum, proj_bias_sum, attn_sum_w, attn...  55.8 us
    all_gather x2, blocking collectives, backward_block(): grad_normed_b = lax.all_gather(grad_cols, 'tensor', axis=1, tiled=True)  37.9 us
    psum x1, blocking collectives, on_device(): lax.psum((scale_sum, shift_sum, proj_sum, proj_bias_sum, attn_sum_w, attn...  17.9 us
  transfers between devices with their start and end apart: 18, of which 16 were waited for; matrix products, arithmetic and copies ran while one was open for 10% of the time, Pallas kernels for 0%

profile of v1, /device:TPU:0, one launch (start us, length us, event | category | flops | bytes accessed | tf_op | source)
XLA Modules:
  0.0 808.0 jit_solution(6514185145795448324)
XLA Ops:
  18.0 52.4 %all-gather.7.cloned.1.call-done = f32[4,197,768]{2,1,0:T(8,128)} async-done(((f32[1,197,768]{2,1,0:T(8,128)}), f32[4,197,768]{2,1,0:T(8,128)}) %all-gather.7.cloned.1.call-update) | async-done | bytes 2420752 | tf_op jit(solution)/shard_map/all_gather | solution.py:136
  79.1 4.2 all-to-all-start
  83.4 12.5 %all-to-all-done = bf16[4,148,768]{2,1,0:T(8,128)(2,1)} async-done(((bf16[4,148,768]{2,1,0:T(8,128)(2,1)}), bf16[4,148,768]{2,1,0:T(8,128)(2,1)}, u32[]{:S(2)}, u32[]{:S(2)}) %all-to-all-start) | async-done | bytes 909344 | tf_op jit(solution)/shard_map/all_to_all | solution.py:151
  101.9 4.3 copy.142
  106.2 4.5 reshape.725
  111.5 39.0 %reduce-scatter.13.cloned.1.call-done = f32[192,592]{1,0:T(8,128)} async-done(((f32[768,592]{1,0:T(8,128)}), f32[192,592]{1,0:T(8,128)}) %reduce-scatter.13.cloned.1.call-update) | async-done | bytes 454672
  154.7 29.3 %all_gather.26 = bf16[4,148,768]{1,0,2:T(4,128)(2,1)} all-gather(bf16[4,148,192]{1,0,2:T(4,128)(2,1)S(1)} %copy.93), channel_id=1, replica_groups=mesh['section'=2,'expert'=4,'tensor'=4] {'tensor'}, dimensions={2}, use_global_device_ids=true | all-gather | bytes 1136640 | tf_op jit(solution)/shard_map/all_gather | solution.py:163
  184.0 3.5 copy.94
  187.5 4.4 all-to-all-start.1
  192.8 10.1 %all-to-all-done.1 = bf16[4,148,768]{2,1,0:T(8,128)(2,1)} async-done(((bf16[4,148,768]{2,1,0:T(8,128)(2,1)}), bf16[4,148,768]{2,1,0:T(8,128)(2,1)}, u32[]{:S(2)}, u32[]{:S(2)}) %all-to-all-start.1) | async-done | bytes 909344 | tf_op jit(solution)/shard_map/all_to_all | solution.py:164
  219.9 52.4 %all-gather.9.cloned.1.call-done = f32[4,197,768]{2,1,0:T(8,128)} async-done(((f32[1,197,768]{2,1,0:T(8,128)}), f32[4,197,768]{2,1,0:T(8,128)}) %all-gather.9.cloned.1.call-update) | async-done | bytes 2420752 | tf_op jit(solution)/shard_map/all_gather | solution.py:136
  281.9 4.8 all-to-all-start.2
  288.3 3.0 mul.457
  291.4 3.3 scatter_custom_fusion.2
  295.8 3.4 all-to-all-done.2
  299.2 3.5 all-to-all-start.4
  302.8 4.6 multiply_convert_fusion
  307.4 7.3 all-to-all-done.4
  314.7 5.2 fusion.127
  323.0 4.3 copy.146
  327.3 4.5 reshape.729
  332.5 4.4 fusion.28
  336.9 4.3 copy.144
  341.2 4.5 reshape.727
  345.7 25.9 %reduce-scatter.17.cloned.1.call-done = f32[192,592]{1,0:T(8,128)} async-done(((f32[768,592]{1,0:T(8,128)}), f32[192,592]{1,0:T(8,128)}) %reduce-scatter.17.cloned.1.call-update) | async-done | bytes 454672
  374.0 4.1 all-to-all-start.5
  378.1 37.0 %reduce-scatter.15.cloned.1.call-done = f32[192,592]{1,0:T(8,128)} async-done(((f32[768,592]{1,0:T(8,128)}), f32[192,592]{1,0:T(8,128)}) %reduce-scatter.15.cloned.1.call-update) | async-done | bytes 454672
  419.3 29.3 %all_gather.29 = bf16[4,148,768]{1,0,2:T(4,128)(2,1)} all-gather(bf16[4,148,192]{1,0,2:T(4,128)(2,1)S(1)} %copy.96), channel_id=1, replica_groups=mesh['section'=2,'expert'=4,'tensor'=4] {'tensor'}, dimensions={2}, use_global_device_ids=true | all-gather | bytes 1136640 | tf_op jit(solution)/shard_map/all_gather | solution.py:163
  448.6 3.5 copy.97
  452.2 4.3 all-to-all-start.3
  462.6 19.6 %all_gather.30 = f32[197,768]{0,1:T(8,128)S(1)} all-gather(f32[197,192]{0,1:T(8,128)S(1)} %copy.100), channel_id=1, replica_groups=mesh['section'=2,'expert'=4,'tensor'=4] {'tensor'}, dimensions={1}, use_global_device_ids=true | all-gather | bytes 756480 | tf_op jit(solution)/shard_map/all_gather | solution.py:253
  500.9 39.6 %all-reduce.7.cloned.1.call-done = f32[197,768]{1,0:T(8,128)} async-done(((f32[197,768]{1,0:T(8,128)}), f32[197,768]{1,0:T(8,128)}) %all-reduce.7.cloned.1.call-update) | async-done | bytes 605200 | tf_op jit(solution)/shard_map/psum | solution.py:281
  549.9 3.0 mul.490
  552.9 4.0 scatter_custom_fusion.3
  559.1 17.6 %all_to_all.40 = bf16[4,148,768]{2,1,0:T(8,128)(2,1)S(1)} all-to-all(bf16[4,148,768]{2,1,0:T(8,128)(2,1)} %reshape.622), channel_id=1, replica_groups=mesh['section'=2,'expert'=4,'tensor'=4] {'expert'}, dimensions={0} | all-to-all | bytes 1818624 | tf_op jit(solution)/shard_map/all_to_all | solution.py:230
  576.8 4.9 fusion.128
  584.8 4.3 copy.148
  589.1 4.5 reshape.731
  595.0 4.1 fusion.61
  601.0 32.2 %reduce-scatter.19.cloned.1.call-done = f32[192,592]{1,0:T(8,128)} async-done(((f32[768,592]{1,0:T(8,128)}), f32[192,592]{1,0:T(8,128)}) %reduce-scatter.19.cloned.1.call-update) | async-done | bytes 454672
  635.6 3.7 all-to-all-start.7
  653.3 18.3 %all_gather.31 = f32[197,768]{0,1:T(8,128)} all-gather(f32[197,192]{0,1:T(8,128)} %copy.107), channel_id=1, replica_groups=mesh['section'=2,'expert'=4,'tensor'=4] {'tensor'}, dimensions={1}, use_global_device_ids=true | all-gather | bytes 756480 | tf_op jit(solution)/shard_map/all_gather | solution.py:253
  684.1 4.1 fusion.129
  692.7 4.3 fusion
  697.0 3.9 fusion.1
  701.3 18.2 %all-reduce.9.cloned.1.call-done = f32[197,768]{1,0:T(8,128)} async-done(((f32[197,768]{1,0:T(8,128)}), f32[197,768]{1,0:T(8,128)}) %all-reduce.9.cloned.1.call-update) | async-done | bytes 605200 | tf_op jit(solution)/shard_map/psum | solution.py:281
  723.7 17.9 %all-reduce.1 = (f32[1,2,768]{2,1,0:T(2,128)}, f32[1,2,768]{2,1,0:T(2,128)}, f32[1,2,192]{2,1,0:T(2,128)}, f32[1,768]{1,0:T(1,128)}) all-reduce(f32[1,2,768]{2,1,0:T(2,128)S(1)} %fusion.104, f32[1,2,768]{2,1,0:T(2,128)S(1)} %fusion.105, f32[1,2,192]{2,1,0:T(2,128)S(1)} %fusion.106, ...), channel_id=1, replica_groups=mesh['section'=2,'expert'=4,'tensor'=4] {'expert'}, use_global_device_ids=true, to_apply=%region_41.42 | all-reduce | flops 4224 | bytes 33792 | tf_op jit(solution)/shard_map/psum | solution.py:373
  741.6 55.8 %all-reduce.11.cloned.1.call-done = (f32[1,768,3,192]{1,3,2,0:T(8,128)}, f32[1,192,768]{2,1,0:T(8,128)}) async-done(((f32[1,768,3,192]{1,3,2,0:T(8,128)}, f32[1,192,768]{2,1,0:T(8,128)}), (f32[1,768,3,192]{1,3,2,0:T(8,128)}, f32[1,192,768]{2,1,0:T(8,128)})) %all-reduce.11.cloned.1.call-update) | async-done | bytes 2359312 | tf_op jit(solution)/shard_map/psum | solution.py:373
  (436 shorter events, 153.9 us)
Async XLA Ops:
  7.2 88.7 %copy-start = (bf16[1,1,768,768]{3,2,1,0:T(8,128)(2,1)S(1)}, bf16[1,1,768,768]{3,2,1,0:T(8,128)(2,1)}, u32[]{:S(2)}) copy-start(bf16[1,1,768,768]{3,2,1,0:T(8,128)(2,1)} %param.22) | copy-start | bytes 3538948
  7.2 63.2 %all-gather.7.cloned.1.call-start = ((), (), s32[]{:S(2)}) async-start(), calls=%async_computation.14 | async-start | bytes 3072000 | tf_op jit(solution)/shard_map/all_gather | solution.py:136
  13.6 203.8 %copy-start.65 = (f32[3,64]{1,0:T(4,128)}, f32[3,64]{1,0:T(4,128)S(1)}, u32[]{:S(2)}) copy-start(f32[3,64]{1,0:T(4,128)S(1)} %add.378) | copy-start | bytes 2308
  15.6 56.7 %copy-start.2 = (f32[1,197,768]{2,0,1:T(1,128)S(1)}, f32[1,197,768]{2,0,1:T(1,128)}, u32[]{:S(2)}) copy-start(f32[1,197,768]{2,0,1:T(1,128)} %param.14) | copy-start | bytes 1815556
  18.0 57.0 %copy-start.95 = (s32[394,1]{0,1:T(1,128)}, s32[394,1]{0,1:T(1,128)S(1)}, u32[]{:S(2)}) copy-start(s32[394,1]{0,1:T(1,128)S(1)} %compare_select_fusion) | copy-start | bytes 4732
  72.5 5.5 copy-start.71
  72.7 5.3 copy-start.87
  78.0 5.4 copy-start.105
  79.1 16.8 %all-to-all-start = ((bf16[4,148,768]{2,1,0:T(8,128)(2,1)}), bf16[4,148,768]{2,1,0:T(8,128)(2,1)}, u32[]{:S(2)}, u32[]{:S(2)}) async-start(bf16[4,148,768]{2,1,0:T(8,128)(2,1)} %reshape.612), calls=%async_computation | async-start | bytes 1867776 | tf_op jit(solution)/shard_map/all_to_all | solution.py:151
  83.3 67.2 %reduce-scatter.13.cloned.1.call-start = ((), (), s32[]{:S(2)}) async-start(), calls=%async_computation.16 | async-start | bytes 2457600
  83.4 14.7 %copy-start.101 = (f32[768]{0:T(1024)}, f32[768]{0:T(1024)S(1)}, u32[]{:S(2)}) copy-start(f32[768]{0:T(1024)S(1)} %reduce.20) | copy-start | bytes 9220
  111.5 43.2 %copy-start.89 = (f32[1,1,192]{2,1,0:T(1,128)}, f32[1,1,192]{2,1,0:T(1,128)S(1)}, u32[]{:S(2)}) copy-start(f32[1,1,192]{2,1,0:T(1,128)S(1)} %constant_dynamic-slice_fusion) | copy-start | bytes 2308
  184.0 8.0 copy-start.93
  184.0 8.8 %copy-start.96 = (s32[394,1]{0,1:T(1,128)S(1)}, s32[394,1]{0,1:T(1,128)}, u32[]{:S(2)}) copy-start(s32[394,1]{0,1:T(1,128)} %copy-done.95) | copy-start | bytes 4732
  187.5 15.4 %all-to-all-start.1 = ((bf16[4,148,768]{2,1,0:T(8,128)(2,1)}), bf16[4,148,768]{2,1,0:T(8,128)(2,1)}, u32[]{:S(2)}, u32[]{:S(2)}) async-start(bf16[4,148,768]{2,1,0:T(8,128)(2,1)} %copy.94), calls=%async_computation.1 | async-start | bytes 1867776 | tf_op jit(solution)/shard_map/all_to_all | solution.py:164
  192.0 80.3 %all-gather.9.cloned.1.call-start = ((), (), s32[]{:S(2)}) async-start(), calls=%async_computation.15 | async-start | bytes 3072000 | tf_op jit(solution)/shard_map/all_gather | solution.py:136
  212.7 3.1 collective-permute-start
  274.4 6.3 copy-start.73
  280.7 5.9 copy-start.94
  281.9 17.3 %all-to-all-start.2 = ((bf16[4,148,768]{2,1,0:T(8,128)(2,1)}), bf16[4,148,768]{2,1,0:T(8,128)(2,1)}, u32[]{:S(2)}, u32[]{:S(2)}) async-start(bf16[4,148,768]{2,1,0:T(8,128)(2,1)} %reshape.616), calls=%async_computation.2 | async-start | bytes 1867776 | tf_op jit(solution)/shard_map/all_to_all | solution.py:151
  299.2 15.4 %all-to-all-start.4 = ((bf16[4,148,768]{2,1,0:T(8,128)(2,1)}), bf16[4,148,768]{2,1,0:T(8,128)(2,1)S(1)}, u32[]{:S(2)}, u32[]{:S(2)}) async-start(bf16[4,148,768]{2,1,0:T(8,128)(2,1)} %reshape.618), calls=%async_computation.4 | async-start | bytes 1867776 | tf_op jit(solution)/shard_map/all_to_all | solution.py:230
  302.7 68.9 %reduce-scatter.17.cloned.1.call-start = ((), (), s32[]{:S(2)}) async-start(), calls=%async_computation.18 | async-start | bytes 2457600
  331.8 83.3 %reduce-scatter.15.cloned.1.call-start = ((), (), s32[]{:S(2)}) async-start(), calls=%async_computation.17 | async-start | bytes 2457600
  373.0 44.9 %copy-start.90 = (f32[1,1,192]{2,1,0:T(1,128)S(1)}, f32[1,1,192]{2,1,0:T(1,128)}, u32[]{:S(2)}) copy-start(f32[1,1,192]{2,1,0:T(1,128)} %copy-done.89) | copy-start | bytes 2308
  374.0 78.2 %all-to-all-start.5 = ((bf16[4,148,192]{2,1,0:T(8,128)(2,1)}), bf16[4,148,192]{2,1,0:T(8,128)(2,1)}, u32[]{:S(2)}, u32[]{:S(2)}) async-start(bf16[4,148,192]{2,1,0:T(8,128)(2,1)} %copy.147), calls=%async_computation.5 | async-start | bytes 622592 | tf_op jit(solution)/shard_map/all_to_all | solution.py:250
  448.6 8.0 copy-start.31
  448.6 8.0 copy-start.51
  448.6 8.0 copy-start.53
  448.6 8.0 copy-start.66
  452.2 31.0 %all-to-all-start.3 = ((bf16[4,148,768]{2,1,0:T(8,128)(2,1)}), bf16[4,148,768]{2,1,0:T(8,128)(2,1)}, u32[]{:S(2)}, u32[]{:S(2)}) async-start(bf16[4,148,768]{2,1,0:T(8,128)(2,1)} %copy.97), calls=%async_computation.3 | async-start | bytes 1867776 | tf_op jit(solution)/shard_map/all_to_all | solution.py:164
  456.5 84.0 %all-reduce.7.cloned.1.call-start = ((), (), s32[]{:S(2)}) async-start(), calls=%async_computation.12 | async-start | bytes 1228800 | tf_op jit(solution)/shard_map/psum | solution.py:281
  487.2 5.8 copy-start.4
  487.2 5.8 copy-start.72
  487.2 5.8 copy-start.74
  487.2 5.8 copy-start.80
  487.2 5.8 copy-start.84
  498.0 42.5 %copy-start.70 = (f32[197]{0:T(256)S(1)}, f32[197]{0:T(256)}, u32[]{:S(2)}) copy-start(f32[197]{0:T(256)} %copy-done.69) | copy-start | bytes 2368
  498.0 42.5 %copy-start.77 = (f32[197]{0:T(256)S(1)}, f32[197]{0:T(256)}, u32[]{:S(2)}) copy-start(f32[197]{0:T(256)} %copy-done.76) | copy-start | bytes 2368
  500.8 132.4 %reduce-scatter.19.cloned.1.call-start = ((), (), s32[]{:S(2)}) async-start(), calls=%async_computation.19 | async-start | bytes 2457600
  543.6 9.2 %copy-start.25 = (f32[197,768]{1,0:T(8,128)}, f32[197,768]{1,0:T(8,128)S(1)}, u32[]{:S(2)}) copy-start(f32[197,768]{1,0:T(8,128)S(1)} %multiply_add_fusion.4) | copy-start | bytes 1815556
  543.6 3.9 collective-permute-start.1
  556.8 19.9 %copy-start.103 = (f32[768]{0:T(1024)S(1)}, f32[768]{0:T(1024)}, u32[]{:S(2)}) copy-start(f32[768]{0:T(1024)} %copy-done.101) | copy-start | bytes 9220
  559.1 17.7 %copy-start.108 = (bf16[1,1,768,768]{3,2,1,0:T(8,128)(2,1)S(1)}, bf16[1,1,768,768]{3,2,1,0:T(8,128)(2,1)}, u32[]{:S(2)}) copy-start(bf16[1,1,768,768]{3,2,1,0:T(8,128)(2,1)} %param.24) | copy-start | bytes 3538948
  635.6 9.2 %all-to-all-start.7 = ((bf16[4,148,192]{2,1,0:T(8,128)(2,1)}), bf16[4,148,192]{2,1,0:T(8,128)(2,1)S(1)}, u32[]{:S(2)}, u32[]{:S(2)}) async-start(bf16[4,148,192]{2,1,0:T(8,128)(2,1)} %copy.149), calls=%async_computation.7 | async-start | bytes 622592 | tf_op jit(solution)/shard_map/all_to_all | solution.py:250
  639.3 80.2 %all-reduce.9.cloned.1.call-start = ((), (), s32[]{:S(2)}) async-start(), calls=%async_computation.13 | async-start | bytes 1228800 | tf_op jit(solution)/shard_map/psum | solution.py:281
  647.4 26.4 %copy-start.8 = (f32[197,768]{1,0:T(8,128)S(1)}, f32[197,768]{1,0:T(8,128)}, u32[]{:S(2)}) copy-start(f32[197,768]{1,0:T(8,128)} %copy-done.7) | copy-start | bytes 1815556
  680.8 116.5 %all-reduce.11.cloned.1.call-start = ((), (), s32[]{:S(2)}) async-start(), calls=%async_computation.20 | async-start | bytes 4718592 | tf_op jit(solution)/shard_map/psum | solution.py:373
  700.9 19.9 %copy-start.81 = (f32[197]{0:T(256)S(1)}, f32[197]{0:T(256)}, u32[]{:S(2)}) copy-start(f32[197]{0:T(256)} %get-tuple-element.115) | copy-start | bytes 2368
  (85 other events, 226.4 us)
Sparse Core Ops, SparseCore 0:
  15.7 54.6 all-gather.6
  110.9 39.6 reduce-scatter.12
  220.0 52.2 all-gather.8
  332.0 39.6 reduce-scatter.16
  374.4 40.6 reduce-scatter.14
  501.0 39.4 all-reduce.6
  593.7 39.4 reduce-scatter.18
  680.9 38.4 all-reduce.8
  723.2 74.1 all-reduce.10
